TPU v7x, 128 devices: a whole 4x4x4 slice. The times are simulated.
128 devices in a mesh: dp: 8 (over y, core), adapter: 16 (over x, z).
Axes of the slice: x: 4, y: 4, z: 4, core: 2. Of those that a mesh axis runs over, the one named last changes fastest.
Arguments:
- activations: bfloat16 [8192, 28672], P('adapter', 'dp'), may hold values from -6 to 6
- cotangent: bfloat16 [8192, 8192], P('adapter', 'dp'), may hold values from -6 to 6
- factor_in: bfloat16 [512, 16, 28672], P('adapter', None, 'dp'), may hold values from -0.03125 to 0.03125
- factor_out: bfloat16 [512, 16, 8192], P('adapter', None, 'dp'), may hold values from -0.0625 to 0.0625
- adapter_ids: int32 [32, 8], P('adapter'), may hold values from 0 to 511, as said below
- router_weights: float32 [32, 8], P('adapter'), may hold values from 0.25 to 1
Outputs:
- input_grad: float32 [8192, 28672], P('adapter', 'dp')
- grad_factor_in: bfloat16 [512, 16, 28672], P('adapter', None, 'dp')
- grad_factor_out: bfloat16 [512, 16, 8192], P('adapter', None, 'dp')
- router_grad: float32 [32, 8], P('adapter')
Inputs may be any that keep to these rules, and one draw needn't show every extreme that they name: `adapter_ids`: the 8 adapters of a request are different. The owner of adapter e is e // 32. Requests are taken in aligned groups of 2 (those of one index of adapter); among the 16 adapters named by one group no owner holds more than 2, and in every group some owner holds exactly 2.
All inputs are finite; a program needn't handle non-finite values.
Results may differ from a plain program's by a relative error of at most 0.012.
Values may be sent and summed in bfloat16 or wider, within the bound.
A program may use at most 128 MiB of HBM per device.

v0:
```python
import jax
import jax.numpy as jnp
from jax import lax
from jax.sharding import PartitionSpec as P

CAP = 2


def body(activations, cotangent, factor_in, factor_out, adapter_ids, router_weights):
    owner_count = lax.axis_size("adapter")
    my_index = lax.axis_index("adapter")
    exp_count = factor_in.shape[0]
    rank_width = factor_in.shape[1]
    req_count = adapter_ids.shape[0]
    top_count = adapter_ids.shape[1]
    pair_count = req_count * top_count
    length = activations.shape[0] // req_count
    slot_count = owner_count * CAP
    my_pairs = adapter_ids.reshape(pair_count)
    my_owner = my_pairs // exp_count
    before = jnp.arange(pair_count)[:, None] > jnp.arange(pair_count)[None, :]
    my_slot = jnp.sum((my_owner[:, None] == my_owner[None, :]) & before, axis=1)
    target = my_owner * CAP + my_slot
    picker = target[:, None] == jnp.arange(slot_count)[None, :]
    all_ids = lax.all_gather(adapter_ids, "adapter", axis=0, tiled=True).reshape(
        owner_count, pair_count
    )
    all_owner = all_ids // exp_count
    all_slot = jnp.sum(
        (all_owner[:, :, None] == all_owner[:, None, :]) & before[None, :, :], axis=2
    )
    is_mine = all_owner == my_index
    local_idx = all_ids - my_index * exp_count
    matches = (
        is_mine[:, :, None, None]
        & (all_slot[:, :, None, None] == jnp.arange(CAP)[None, None, :, None])
        & (local_idx[:, :, None, None] == jnp.arange(exp_count)[None, None, None, :])
    )
    selector = jnp.any(matches, axis=1)
    selector = selector.astype(jnp.bfloat16)
    send_in = jnp.einsum(
        "jce,erf->jcrf", selector, factor_in, preferred_element_type=jnp.float32
    ).astype(jnp.bfloat16)
    send_out = jnp.einsum(
        "jce,erd->jcrd", selector, factor_out, preferred_element_type=jnp.float32
    ).astype(jnp.bfloat16)
    rows_in = activations.reshape(req_count, length, -1)
    rows_out = cotangent.reshape(req_count, length, -1)
    picker_bf = picker.astype(jnp.bfloat16)
    got_in, got_out = (
        lax.all_to_all(send_in, "adapter", split_axis=0, concat_axis=0, tiled=True),
        lax.all_to_all(send_out, "adapter", split_axis=0, concat_axis=0, tiled=True),
    )
    got_in = got_in.reshape(slot_count, rank_width, -1)
    got_out = got_out.reshape(slot_count, rank_width, -1)
    pair_in = jnp.einsum(
        "qs,srf->qrf", picker_bf, got_in, preferred_element_type=jnp.float32
    ).astype(jnp.bfloat16)
    pair_out = jnp.einsum(
        "qs,srd->qrd", picker_bf, got_out, preferred_element_type=jnp.float32
    ).astype(jnp.bfloat16)
    pair_in = pair_in.reshape(req_count, top_count * rank_width, -1)
    pair_out = pair_out.reshape(req_count, top_count * rank_width, -1)
    part_proj = jnp.einsum("blf,bjf->blj", rows_in, pair_in, preferred_element_type=jnp.float32)
    part_pull = jnp.einsum("bld,bjd->blj", rows_out, pair_out, preferred_element_type=jnp.float32)
    projected, pulled = lax.psum((part_proj, part_pull), "dp")
    router_grad = jnp.sum(
        (projected * pulled).reshape(req_count, length, top_count, rank_width), axis=(1, 3)
    )
    row_scale = jnp.repeat(router_weights, rank_width, axis=1)
    pulled_weighted = (pulled * row_scale[:, None, :]).astype(jnp.bfloat16)
    projected_weighted = (projected * row_scale[:, None, :]).astype(jnp.bfloat16)
    input_grad = jnp.einsum(
        "blj,bjf->blf", pulled_weighted, pair_in, preferred_element_type=jnp.float32
    ).reshape(req_count * length, -1)
    term_in = jnp.einsum(
        "blj,blf->bjf", pulled_weighted, rows_in, preferred_element_type=jnp.float32
    ).astype(jnp.bfloat16)
    term_out = jnp.einsum(
        "blj,bld->bjd", projected_weighted, rows_out, preferred_element_type=jnp.float32
    ).astype(jnp.bfloat16)
    back_in = jnp.einsum(
        "qs,qrf->srf",
        picker_bf,
        term_in.reshape(pair_count, rank_width, -1),
        preferred_element_type=jnp.float32,
    ).astype(jnp.bfloat16)
    back_out = jnp.einsum(
        "qs,qrd->srd",
        picker_bf,
        term_out.reshape(pair_count, rank_width, -1),
        preferred_element_type=jnp.float32,
    ).astype(jnp.bfloat16)
    back_in = back_in.reshape(owner_count, CAP, rank_width, -1)
    back_out = back_out.reshape(owner_count, CAP, rank_width, -1)
    ret_in, ret_out = (
        lax.all_to_all(back_in, "adapter", split_axis=0, concat_axis=0, tiled=True),
        lax.all_to_all(back_out, "adapter", split_axis=0, concat_axis=0, tiled=True),
    )
    grad_factor_in = jnp.einsum(
        "jce,jcrf->erf", selector, ret_in, preferred_element_type=jnp.float32
    ).astype(jnp.bfloat16)
    grad_factor_out = jnp.einsum(
        "jce,jcrd->erd", selector, ret_out, preferred_element_type=jnp.float32
    ).astype(jnp.bfloat16)
    return (input_grad, grad_factor_in, grad_factor_out, router_grad)


def solution(mesh):
    return jax.shard_map(
        body,
        mesh=mesh,
        in_specs=(
            P("adapter", "dp"),
            P("adapter", "dp"),
            P("adapter", None, "dp"),
            P("adapter", None, "dp"),
            P("adapter", None),
            P("adapter", None),
        ),
        out_specs=(
            P("adapter", "dp"),
            P("adapter", None, "dp"),
            P("adapter", None, "dp"),
            P("adapter", None),
        ),
        check_vma=False,
    )
```

profile of v0, /device:TPU:124, one launch (start us, length us, event | category | flops | bytes accessed | tf_op | source)
XLA Modules:
  0.0 286.8 jit_solution(15268726753402709077)
XLA Ops:
  7.2 0.0 copy-start
  7.2 21.6 %all-gather = s32[16,2,8]{2,1,0:T(2,128)S(1)} all-gather(s32[1,2,8]{2,1,0:T(2,128)} %bitcast.82), channel_id=1, replica_groups=mesh['dp'=8,'adapter'=16] {'adapter'}, dimensions={0}, use_global_device_ids=true | all-gather | bytes 1088 | tf_op jit(solution)/shard_map/all_gather | solution.py:25
  28.8 0.1 copy.61
  28.9 0.1 copy.65
  28.9 0.1 copy.62
  29.0 0.1 copy.63
  29.1 0.1 iota_compare_fusion
  29.2 0.4 convert_reduce_fusion
  29.7 0.2 and_reduce_fusion
  29.8 2.7 convolution_convert_fusion.4
  32.5 1.5 copy.68
  34.1 6.9 %all-to-all-start = ((bf16[16,2,16,1024]{3,2,1,0:T(8,128)(2,1)}), bf16[16,2,16,1024]{3,2,1,0:T(8,128)(2,1)S(1)}, u32[]{:S(2)}, u32[]{:S(2)}) async-start(bf16[16,2,16,1024]{3,2,1,0:T(8,128)(2,1)} %copy.68), calls=%async_computation | async-start | bytes 2097152 | tf_op jit(solution)/shard_map/all_to_all | solution.py:52
  41.0 6.9 %convolution_convert_fusion = bf16[16,2,16,3584]{3,0,2,1:T(8,128)(2,1)S(1)} fusion(bf16[32,16,3584]{2,1,0:T(8,128)(2,1)} %param.8, pred[16,2,32,1]{2,1,0,3:T(4,128)(4,1)S(1)} %bitcast.81), kind=kOutput, calls=%fused_computation.1 | convolution fusion | flops 119275520 | bytes 7341056 | tf_op jit(solution)/shard_map/jce,erf->jcrf/dot_general | solution.py:41
  47.9 3.8 %copy.73 = bf16[16,2,16,3584]{3,2,1,0:T(8,128)(2,1)} copy(bf16[16,2,16,3584]{3,0,2,1:T(8,128)(2,1)S(1)} %convolution_convert_fusion) | data formatting | bytes 7340032 | tf_op jit(solution)/shard_map/convert_element_type | solution.py:43
  51.7 7.4 %all-to-all-start.1 = ((bf16[16,2,16,3584]{3,2,1,0:T(8,128)(2,1)}), bf16[16,2,16,3584]{3,2,1,0:T(8,128)(2,1)}, u32[]{:S(2)}, u32[]{:S(2)}) async-start(bf16[16,2,16,3584]{3,2,1,0:T(8,128)(2,1)} %copy.73), calls=%async_computation.1 | async-start | bytes 7340032 | tf_op jit(solution)/shard_map/all_to_all | solution.py:51
  59.1 0.2 all-reduce.3.cloned.1.call-start
  59.3 0.1 reshape.240
  59.4 0.2 convert_reduce_fusion.1
  59.6 1.2 convolution_convert_fusion.7
  60.9 0.3 copy.70
  61.2 1.2 convolution_bitcast_fusion.1
  62.4 39.2 %all-to-all-done.1 = bf16[16,2,16,3584]{3,2,1,0:T(8,128)(2,1)} async-done(((bf16[16,2,16,3584]{3,2,1,0:T(8,128)(2,1)}), bf16[16,2,16,3584]{3,2,1,0:T(8,128)(2,1)}, u32[]{:S(2)}, u32[]{:S(2)}) %all-to-all-start.1) | async-done | bytes 3670048 | tf_op jit(solution)/shard_map/all_to_all | solution.py:51
  101.6 6.2 %convolution_convert_fusion.3 = bf16[16,16,3584]{2,0,1:T(8,128)(2,1)S(1)} fusion(bf16[32,16,3584]{2,1,0:T(8,128)(2,1)} %bitcast.11, s32[16]{0:T(128)S(1)} %multiply_add_fusion), kind=kOutput, calls=%fused_computation.4 | convolution fusion | flops 59638272 | bytes 5505088 | tf_op jit(solution)/shard_map/qs,srf->qrf/dot_general | solution.py:56
  107.8 1.0 copy.75
  108.8 2.0 convolution_bitcast_fusion
  110.8 0.0 all-reduce.3.cloned.1.call-update
  110.9 0.1 broadcast_in_dim.2
  110.9 0.1 mul.31
  111.0 61.1 %all-reduce.3.cloned.1.call-done = (f32[2,256,128]{1,2,0:T(8,128)}, f32[2,256,128]{1,2,0:T(8,128)}) async-done(((f32[2,256,128]{1,2,0:T(8,128)}, f32[2,256,128]{1,2,0:T(8,128)}), (f32[2,256,128]{1,2,0:T(8,128)}, f32[2,256,128]{1,2,0:T(8,128)})) %all-reduce.3.cloned.1.call-update) | async-done | bytes 524304 | tf_op jit(solution)/shard_map/psum | solution.py:66
  172.1 1.3 convolution_convert_fusion.6
  173.5 0.6 convolution_convert_fusion.5
  174.0 1.2 reshape.252
  175.3 3.2 %copy.82 = bf16[16,2,16,1024]{3,1,2,0:T(2,128)(2,1)} copy(bf16[16,2,16,1024]{3,1,0,2:T(2,128)(2,1)} %reshape.252) | data formatting | bytes 2097152 | tf_op jit(solution)/shard_map/reshape | solution.py:95
  178.4 7.1 %all-to-all-start.3 = ((bf16[16,2,16,1024]{3,1,2,0:T(2,128)(2,1)}), bf16[16,2,16,1024]{3,1,2,0:T(2,128)(2,1)S(1)}, u32[]{:S(2)}, u32[]{:S(2)}) async-start(bf16[16,2,16,1024]{3,1,2,0:T(2,128)(2,1)} %copy.82), calls=%async_computation.3 | async-start | bytes 2097152 | tf_op jit(solution)/shard_map/all_to_all | solution.py:98
  185.6 2.7 convolution_convert_fusion.2
  188.3 4.2 %convolution_convert_fusion.1 = bf16[32,16,3584]{2,0,1:T(8,128)(2,1)} fusion(bf16[16,16,3584]{2,1,0:T(8,128)(2,1)S(1)} %bitcast.76, s32[16]{0:T(128)S(1)} %multiply_add_fusion), kind=kOutput, calls=%fused_computation.2 | convolution fusion | flops 60555776 | bytes 5505088 | tf_op jit(solution)/shard_map/qs,qrf->srf/dot_general | solution.py:82
  192.5 8.1 %reshape.250 = bf16[16,2,16,3584]{3,1,0,2:T(2,128)(2,1)} reshape(bf16[32,16,3584]{2,0,1:T(8,128)(2,1)} %convolution_convert_fusion.1) | data formatting | bytes 7340032 | tf_op jit(solution)/shard_map/reshape | solution.py:94
  200.6 7.3 %copy.78 = bf16[16,2,16,3584]{3,1,2,0:T(2,128)(2,1)} copy(bf16[16,2,16,3584]{3,1,0,2:T(2,128)(2,1)} %reshape.250) | data formatting | bytes 7340032 | tf_op jit(solution)/shard_map/reshape | solution.py:94
  207.8 7.4 %all-to-all-start.2 = ((bf16[16,2,16,3584]{3,1,2,0:T(2,128)(2,1)}), bf16[16,2,16,3584]{3,1,2,0:T(2,128)(2,1)}, u32[]{:S(2)}, u32[]{:S(2)}) async-start(bf16[16,2,16,3584]{3,1,2,0:T(2,128)(2,1)} %copy.78), calls=%async_computation.2 | async-start | bytes 7340032 | tf_op jit(solution)/shard_map/all_to_all | solution.py:97
  215.2 0.1 multiply_reduce_fusion
  215.3 0.1 reduce_sum.37
  215.4 0.7 reduce_sum.38
  216.1 4.3 %fusion.11 = f32[2,256,3584]{2,1,0:T(8,128)} fusion(bf16[2,128,3584]{2,1,0:T(8,128)(2,1)S(1)} %bitcast.72, f32[2,256,128]{1,2,0:T(8,128)S(1)} %copy-done.3, f32[2,128]{1,0:T(2,128)S(1)} %mul.31), kind=kOutput, calls=%fused_computation.29 | convolution fusion | flops 469893120 | bytes 9438208 | tf_op jit(solution)/shard_map/blj,bjf->blf/dot_general | solution.py:73
  220.3 0.7 bitcast_convert_fusion.1
  221.1 1.5 copy.86
  222.6 49.1 %all-to-all-done.2 = bf16[16,2,16,3584]{3,1,2,0:T(2,128)(2,1)} async-done(((bf16[16,2,16,3584]{3,1,2,0:T(2,128)(2,1)}), bf16[16,2,16,3584]{3,1,2,0:T(2,128)(2,1)}, u32[]{:S(2)}, u32[]{:S(2)}) %all-to-all-start.2) | async-done | bytes 3670048 | tf_op jit(solution)/shard_map/all_to_all | solution.py:97
  271.7 4.4 %bitcast_convert_fusion = bf16[32,16,3584]{2,0,1:T(8,128)(2,1)S(1)} fusion(bf16[16,2,16,3584]{3,1,2,0:T(2,128)(2,1)} %all-to-all-done.2, pred[16,2,32]{2,1,0:T(4,128)(4,1)S(1)} %and_reduce_fusion), kind=kOutput, calls=%fused_computation | convolution fusion | flops 119275520 | bytes 7341056 | tf_op jit(solution)/shard_map/jce,jcrf->erf/dot_general | solution.py:100
  276.1 3.8 %copy.85 = bf16[32,16,3584]{2,1,0:T(8,128)(2,1)} copy(bf16[32,16,3584]{2,0,1:T(8,128)(2,1)S(1)} %bitcast_convert_fusion) | data formatting | bytes 7340032
  (21 shorter events, 0.1 us)
Async XLA Ops:
  7.2 54.0 %copy-start = (bf16[512,1024]{1,0:T(8,128)(2,1)S(1)}, bf16[512,1024]{1,0:T(8,128)(2,1)}, u32[]{:S(2)}) copy-start(bf16[512,1024]{1,0:T(8,128)(2,1)} %param.7) | copy-start | bytes 3145732
  34.1 17.7 %all-to-all-start = ((bf16[16,2,16,1024]{3,2,1,0:T(8,128)(2,1)}), bf16[16,2,16,1024]{3,2,1,0:T(8,128)(2,1)S(1)}, u32[]{:S(2)}, u32[]{:S(2)}) async-start(bf16[16,2,16,1024]{3,2,1,0:T(8,128)(2,1)} %copy.68), calls=%async_computation | async-start | bytes 2097152 | tf_op jit(solution)/shard_map/all_to_all | solution.py:52
  51.7 7.6 %copy-start.5 = (s32[2,8]{1,0:T(2,128)S(1)}, s32[2,8]{1,0:T(2,128)}, u32[]{:S(2)}) copy-start(s32[2,8]{1,0:T(2,128)} %param.10) | copy-start | bytes 196
  51.7 49.8 %all-to-all-start.1 = ((bf16[16,2,16,3584]{3,2,1,0:T(8,128)(2,1)}), bf16[16,2,16,3584]{3,2,1,0:T(8,128)(2,1)}, u32[]{:S(2)}, u32[]{:S(2)}) async-start(bf16[16,2,16,3584]{3,2,1,0:T(8,128)(2,1)} %copy.73), calls=%async_computation.1 | async-start | bytes 7340032 | tf_op jit(solution)/shard_map/all_to_all | solution.py:51
  59.1 113.0 %all-reduce.3.cloned.1.call-start = ((), (), s32[]{:S(2)}) async-start(), calls=%async_computation.4 | async-start | bytes 1048576 | tf_op jit(solution)/shard_map/psum | solution.py:66
  101.6 7.2 %copy-start.2 = (bf16[512,3584]{1,0:T(8,128)(2,1)S(1)}, bf16[512,3584]{1,0:T(8,128)(2,1)}, u32[]{:S(2)}) copy-start(bf16[512,3584]{1,0:T(8,128)(2,1)} %param.6) | copy-start | bytes 11010052
  108.8 2.1 copy-start.6
  173.4 12.1 %copy-start.3 = (f32[2,256,128]{1,2,0:T(8,128)S(1)}, f32[2,256,128]{1,2,0:T(8,128)}, u32[]{:S(2)}) copy-start(f32[2,256,128]{1,2,0:T(8,128)} %get-tuple-element.20) | copy-start | bytes 786436
  178.4 29.4 %all-to-all-start.3 = ((bf16[16,2,16,1024]{3,1,2,0:T(2,128)(2,1)}), bf16[16,2,16,1024]{3,1,2,0:T(2,128)(2,1)S(1)}, u32[]{:S(2)}, u32[]{:S(2)}) async-start(bf16[16,2,16,1024]{3,1,2,0:T(2,128)(2,1)} %copy.82), calls=%async_computation.3 | async-start | bytes 2097152 | tf_op jit(solution)/shard_map/all_to_all | solution.py:98
  207.8 7.4 %copy-start.4 = (f32[2,256,128]{1,2,0:T(8,128)S(1)}, f32[2,256,128]{1,2,0:T(8,128)}, u32[]{:S(2)}) copy-start(f32[2,256,128]{1,2,0:T(8,128)} %get-tuple-element.21) | copy-start | bytes 786436
  207.8 63.9 %all-to-all-start.2 = ((bf16[16,2,16,3584]{3,1,2,0:T(2,128)(2,1)}), bf16[16,2,16,3584]{3,1,2,0:T(2,128)(2,1)}, u32[]{:S(2)}, u32[]{:S(2)}) async-start(bf16[16,2,16,3584]{3,1,2,0:T(2,128)(2,1)} %copy.78), calls=%async_computation.2 | async-start | bytes 7340032 | tf_op jit(solution)/shard_map/all_to_all | solution.py:97
  271.7 8.3 %copy-start.1 = (bf16[512,1024]{1,0:T(8,128)(2,1)S(1)}, bf16[512,1024]{1,0:T(8,128)(2,1)}, u32[]{:S(2)}) copy-start(bf16[512,1024]{1,0:T(8,128)(2,1)} %param.7) | copy-start | bytes 3145732
Sparse Core Ops, SparseCore 0:
  111.0 61.1 all-reduce.2
where the time goes:
time: 288 us; the launch traced here: 287 us
  waiting for transfers between devices  149 us (52%)
  matrix products  38.3 us (13%)
  local copies, waits for them, and re-layouts  32.5 us (11%)
  starting transfers between devices  29 us (10%)
  blocking collectives  21.6 us (8%)
  between operations  14.2 us (5%)
    psum x1, waiting for transfers between devices, body(): projected, pulled = lax.psum((part_proj, part_pull), 'dp')  61.1 us
    all_to_all x1, waiting for transfers between devices, body(): lax.all_to_all(back_in, 'adapter', split_axis=0, concat_axis=0, tiled=True)  49.1 us
    all_to_all x1, waiting for transfers between devices, body(): lax.all_to_all(send_in, 'adapter', split_axis=0, concat_axis=0, tiled=True)  39.2 us
    all_gather x1, blocking collectives, body(): lax.all_gather(adapter_ids, 'adapter', axis=0, tiled=True)  21.6 us
    reshape x2, local copies, waits for them, and re-layouts, body(): back_in = back_in.reshape(owner_count, CAP, rank_width, -1)  15.4 us
    all_to_all x1, starting transfers between devices, body(): lax.all_to_all(send_in, 'adapter', split_axis=0, concat_axis=0, tiled=True)  7.36 us
    all_to_all x1, starting transfers between devices, body(): lax.all_to_all(back_in, 'adapter', split_axis=0, concat_axis=0, tiled=True)  7.36 us
    all_to_all x1, starting transfers between devices, body(): lax.all_to_all(back_out, 'adapter', split_axis=0, concat_axis=0, tiled=True)  7.14 us
  transfers between devices with their start and end apart: 5, of which 3 were waited for; matrix products, arithmetic and copies ran while one was open for 15% of the time, Pallas kernels for 0%

commit v1 on v0

v1 whole, which is shorter than its diff:
```python
import functools

import jax
import jax.numpy as jnp
from jax import lax
from jax.experimental import pallas as pl
from jax.experimental.pallas import tpu as pltpu
from jax.sharding import PartitionSpec as P

MESH = pl.DeviceIdType.MESH
SIDE = 4
OWNERS = SIDE * SIDE
CAP = 2
RANK = 16
EXP_DEV = 32
DP = 8
ORDER = (
    (1, 1), (3, 3), (1, 3), (3, 1), (2, 0), (0, 2), (2, 2), (2, 1),
    (1, 2), (2, 3), (3, 2), (1, 0), (3, 0), (0, 1), (0, 3),
)


def rot(off):
    return off[0] * SIDE + off[1]


def exchange_kernel(
    slot_of_pair, pair_of_slot,
    tab_ref, scale_ref, fi_hbm, fo_hbm, act_hbm, cot_hbm,
    ret_in, ret_out, pair_in_hbm, pw_out, tab_out, router_out,
    fi, fo, act, cot, send_in, send_out, got_in, got_out, pair_in, pair_out,
    term_in, term_out, back_in, back_out, tab, tab_smem,
    rs_send, rs_got, kept, ag, rp,
    load_sem, out_sem, tab_ss, tab_rs, fo_ss, fo_rs, fi_ss, fi_rs,
    bi_ss, bi_rs, bo_ss, bo_rs, rs_ss, rs_rs, ag_ss, ag_rs, rp_ss, rp_rs,
):
    me = lax.axis_index("adapter")
    mx, mz = me // SIDE, me % SIDE
    dp = lax.axis_index("dp")

    def there(off):
        return {"adapter": ((mx + off[0]) % SIDE) * SIDE + (mz + off[1]) % SIDE}

    def back(off):
        return {"adapter": ((mx + SIDE - off[0]) % SIDE) * SIDE + (mz + SIDE - off[1]) % SIDE}

    def beside(d):
        return {"dp": (dp + d) % DP}

    loads = []
    for i, (src, dst) in enumerate(((fo_hbm, fo), (fi_hbm, fi), (cot_hbm, cot), (act_hbm, act))):
        loads.append(pltpu.make_async_copy(src, dst, load_sem.at[i]))
        loads[-1].start()

    bar = pltpu.get_barrier_semaphore()
    for off in ORDER:
        pl.semaphore_signal(bar, inc=1, device_id=there(off), device_id_type=MESH)
    for d in range(1, DP):
        pl.semaphore_signal(bar, inc=1, device_id=beside(d), device_id_type=MESH)
    pl.semaphore_wait(bar, len(ORDER) + DP - 1)

    def push(src, dst, ss, rs, dev):
        c = pltpu.make_async_remote_copy(
            src_ref=src, dst_ref=dst, send_sem=ss, recv_sem=rs, device_id=dev, device_id_type=MESH
        )
        c.start()
        return c

    tabs = []
    for i, off in enumerate(ORDER):
        j = rot(off)
        tabs.append(push(tab_ref.at[j], tab.at[j], tab_ss.at[i], tab_rs.at[i], back(off)))
    tab[0] = tab_ref[0]
    for c in tabs:
        c.wait()
    local = pltpu.make_async_copy(tab, tab_smem, out_sem.at[0])
    local.start()
    local.wait()

    def pick(src, dst, j, c):
        dst[j * CAP + c] = src[jnp.clip(tab_smem[j, 0, c], 0, EXP_DEV - 1)]

    loads[0].wait()
    fos = []
    for i, off in enumerate(ORDER):
        j = rot(off)
        for c in range(CAP):
            pick(fo, send_out, j, c)
        rows = pl.ds(j * CAP, CAP)
        fos.append(push(send_out.at[rows], got_out.at[rows], fo_ss.at[i], fo_rs.at[i], there(off)))
    for c in range(CAP):
        pick(fo, got_out, 0, c)

    loads[1].wait()
    fis = []
    for c in range(CAP):
        for i, off in enumerate(ORDER):
            j = rot(off)
            pick(fi, send_in, j, c)
            n = c * len(ORDER) + i
            rows = pl.ds(j * CAP + c, 1)
            fis.append(push(send_in.at[rows], got_in.at[rows], fi_ss.at[n], fi_rs.at[n], there(off)))
    for c in range(CAP):
        pick(fi, got_in, 0, c)

    def combine(step):
        cs = []
        for d in range(1, DP):
            cs.append(push(rs_send.at[step, (dp + d) % DP], rs_got.at[step, d],
                           rs_ss.at[step, d], rs_rs.at[step, d], beside(d)))
        total = rs_send[step, dp]
        for c in cs:
            c.wait()
        for d in range(1, DP):
            total = total + rs_got[step, d]
        return total

    def spread(step, total):
        scale = scale_ref[pl.ds(dp // (DP // 2), 1), :]
        ag[step, dp] = (total * scale).astype(jnp.bfloat16)
        return [
            push(ag.at[step, dp], ag.at[step, dp], ag_ss.at[step, d], ag_rs.at[step, d], beside(d))
            for d in range(1, DP)
        ]

    half = DP // 2
    length = act.shape[1]
    top = slot_of_pair.shape[0] // 2
    width = top * RANK
    chunk = length // half

    def project(step, rows, got, pair):
        for b in range(2):
            for k in range(top):
                p = b * top + k
                pair[p] = got[slot_of_pair[p]]
            part = lax.dot_general(
                rows[b], pair[b * top:(b + 1) * top].reshape(width, pair.shape[2]),
                (((1,), (1,)), ((), ())), preferred_element_type=jnp.float32,
            )
            for h in range(half):
                rs_send[step, b * half + h] = part[h * chunk:(h + 1) * chunk]

    def terms(step, rows, term, cols):
        n = rows.shape[2]
        for b in range(2):
            w = ag[step, b * half:(b + 1) * half].reshape(length, width)
            for s in range(0, n, cols):
                t = lax.dot_general(
                    w, rows[b, :, s:s + cols], (((0,), (0,)), ((), ())),
                    preferred_element_type=jnp.float32,
                )
                term[b * top:(b + 1) * top, :, s:s + cols] = t.astype(jnp.bfloat16).reshape(top, RANK, cols)

    for c in fos:
        c.wait()
    loads[2].wait()
    project(0, cot, got_out, pair_out)
    pulled = combine(0)
    kept[...] = pulled
    ags = spread(0, pulled)
    loads[3].wait()
    for c in ags:
        c.wait()

    terms(0, act, term_in, 512)
    bis = []
    for c in range(CAP):
        for i, off in enumerate(ORDER):
            j = rot(off)
            s = j * CAP + c
            back_in[s] = term_in[pair_of_slot[s]]
            n = c * len(ORDER) + i
            rows = pl.ds(s, 1)
            bis.append(push(back_in.at[rows], ret_in.at[rows], bi_ss.at[n], bi_rs.at[n], back(off)))
    for c in range(CAP):
        back_in[c] = term_in[pair_of_slot[c]]
    own = [pltpu.make_async_copy(back_in.at[pl.ds(0, CAP)], ret_in.at[pl.ds(0, CAP)], out_sem.at[0])]
    own[0].start()

    for c in fis:
        c.wait()
    project(1, act, got_in, pair_in)
    own.append(pltpu.make_async_copy(pair_in, pair_in_hbm, out_sem.at[1]))
    own[1].start()
    projected = combine(1)
    ags = spread(1, projected)
    rp[dp] = jnp.broadcast_to(jnp.sum(projected * kept[...], axis=0, keepdims=True), rp.shape[1:])
    rps = [
        push(rp.at[dp], rp.at[dp], rp_ss.at[d], rp_rs.at[d], beside(d)) for d in range(1, DP)
    ]
    for c in ags:
        c.wait()
    terms(1, cot, term_out, 512)
    bos = []
    for i, off in enumerate(ORDER):
        j = rot(off)
        for c in range(CAP):
            back_out[j * CAP + c] = term_out[pair_of_slot[j * CAP + c]]
        rows = pl.ds(j * CAP, CAP)
        bos.append(push(back_out.at[rows], ret_out.at[rows], bo_ss.at[i], bo_rs.at[i], back(off)))
    for c in range(CAP):
        back_out[c] = term_out[pair_of_slot[c]]
    own.append(pltpu.make_async_copy(back_out.at[pl.ds(0, CAP)], ret_out.at[pl.ds(0, CAP)], out_sem.at[2]))
    own[2].start()

    pw_out[...] = ag[0]
    tab_out[...] = tab[...]
    for c in rps:
        c.wait()
    for b in range(2):
        acc = rp[b * half]
        for h in range(1, half):
            acc = acc + rp[b * half + h]
        router_out[b] = acc
    for c in own + bis + bos:
        c.wait()


def finish_kernel(tab, pw, pair_in, ret_in, ret_out, ig, gi, go, place):
    rows = place.shape[0]

    @pl.when(pl.program_id(0) == 0)
    def _():
        r = lax.broadcasted_iota(jnp.int32, (RANK, rows), 0)
        col = lax.broadcasted_iota(jnp.int32, (RANK, rows), 1)
        for s in range(OWNERS * CAP):
            hit = (tab[s // CAP, 0, s % CAP] * RANK + r) == col
            place[s * RANK:(s + 1) * RANK, :] = jnp.where(hit, 1.0, 0.0).astype(jnp.bfloat16)
        go[...] = lax.dot_general(
            place[...], ret_out[...], (((0,), (0,)), ((), ())), preferred_element_type=jnp.float32
        ).astype(jnp.bfloat16)

    gi[...] = lax.dot_general(
        place[...], ret_in[...], (((0,), (0,)), ((), ())), preferred_element_type=jnp.float32
    ).astype(jnp.bfloat16)
    for b in range(2):
        ig[b] = jnp.dot(pw[b], pair_in[b], preferred_element_type=jnp.float32)


def body(activations, cotangent, factor_in, factor_out, adapter_ids, router_weights):
    req, top = adapter_ids.shape
    tokens, ff = activations.shape
    model = cotangent.shape[1]
    length = tokens // req
    pairs = req * top
    slots = OWNERS * CAP
    chunk = tokens // DP
    width = top * RANK
    bf, f32, i32 = jnp.bfloat16, jnp.float32, jnp.int32

    me = lax.axis_index("adapter")
    ids = adapter_ids.reshape(pairs)
    owner = ids // EXP_DEV
    before = jnp.arange(pairs)[:, None] > jnp.arange(pairs)[None, :]
    nth = jnp.sum((owner[:, None] == owner[None, :]) & before, axis=1)
    turn = ((me // SIDE - owner // SIDE) % SIDE) * SIDE + (me - owner) % SIDE
    slot_of_pair = jnp.minimum(turn * CAP + nth, slots - 1).astype(i32)
    hits = slot_of_pair[None, :] == jnp.arange(slots)[:, None]
    pair_of_slot = jnp.max(jnp.where(hits, jnp.arange(pairs)[None, :], 0), axis=1).astype(i32)
    named = jnp.max(jnp.where(hits, (ids % EXP_DEV)[None, :], -1), axis=1).astype(i32)
    tab = jnp.pad(named.reshape(OWNERS, 1, CAP), ((0, 0), (0, 0), (0, 128 - CAP)))
    scale = jnp.repeat(router_weights, RANK, axis=1)

    any_ = pl.BlockSpec(memory_space=pl.ANY)
    smem = pl.BlockSpec(memory_space=pltpu.SMEM)
    vmem = pl.BlockSpec(memory_space=pltpu.VMEM)
    dma = pltpu.SemaphoreType.DMA
    far = OWNERS - 1
    ret_in, ret_out, pair_in, pw, tab_all, router = pl.pallas_call(
        exchange_kernel,
        out_shape=(
            jax.ShapeDtypeStruct((slots, RANK, ff), bf),
            jax.ShapeDtypeStruct((slots, RANK, model), bf),
            jax.ShapeDtypeStruct((pairs, RANK, ff), bf),
            jax.ShapeDtypeStruct((DP, chunk, width), bf),
            jax.ShapeDtypeStruct((OWNERS, 1, 128), i32),
            jax.ShapeDtypeStruct((req, 8, width), f32),
        ),
        in_specs=[smem, smem, vmem, vmem, any_, any_, any_, any_],
        out_specs=(any_, any_, any_, vmem, vmem, vmem),
        scratch_shapes=[
            pltpu.VMEM((EXP_DEV, RANK, ff), bf),
            pltpu.VMEM((EXP_DEV, RANK, model), bf),
            pltpu.VMEM((req, length, ff), bf),
            pltpu.VMEM((req, length, model), bf),
            pltpu.VMEM((slots, RANK, ff), bf),
            pltpu.VMEM((slots, RANK, model), bf),
            pltpu.VMEM((slots, RANK, ff), bf),
            pltpu.VMEM((slots, RANK, model), bf),
            pltpu.VMEM((pairs, RANK, ff), bf),
            pltpu.VMEM((pairs, RANK, model), bf),
            pltpu.VMEM((pairs, RANK, ff), bf),
            pltpu.VMEM((pairs, RANK, model), bf),
            pltpu.VMEM((slots, RANK, ff), bf),
            pltpu.VMEM((slots, RANK, model), bf),
            pltpu.VMEM((OWNERS, 1, 128), i32),
            pltpu.SMEM((OWNERS, 1, 128), i32),
            pltpu.VMEM((2, DP, chunk, width), f32),
            pltpu.VMEM((2, DP, chunk, width), f32),
            pltpu.VMEM((chunk, width), f32),
            pltpu.VMEM((2, DP, chunk, width), bf),
            pltpu.VMEM((DP, 8, width), f32),
            dma((4,)), dma((3,)),
            dma((far,)), dma((far,)),
            dma((far,)), dma((far,)),
            dma((CAP * far,)), dma((CAP * far,)),
            dma((CAP * far,)), dma((CAP * far,)),
            dma((far,)), dma((far,)),
            dma((2, DP)), dma((2, DP)), dma((2, DP)), dma((2, DP)), dma((DP,)), dma((DP,)),
        ],
        compiler_params=pltpu.CompilerParams(
            collective_id=0, has_side_effects=True, vmem_limit_bytes=48 << 20
        ),
        name="exchange",
    )(
        slot_of_pair, pair_of_slot, tab, scale, factor_in, factor_out,
        activations.reshape(req, length, ff), cotangent.reshape(req, length, model),
    )

    cols = 512
    rows = slots * RANK
    input_grad, grad_in, grad_out = pl.pallas_call(
        finish_kernel,
        grid=(ff // cols,),
        out_shape=(
            jax.ShapeDtypeStruct((req, length, ff), f32),
            jax.ShapeDtypeStruct((EXP_DEV * RANK, ff), bf),
            jax.ShapeDtypeStruct((EXP_DEV * RANK, model), bf),
        ),
        in_specs=[
            smem,
            pl.BlockSpec((req, length, width), lambda i: (0, 0, 0)),
            pl.BlockSpec((req, width, cols), lambda i: (0, 0, i)),
            pl.BlockSpec((rows, cols), lambda i: (0, i)),
            pl.BlockSpec((rows, model), lambda i: (0, 0)),
        ],
        out_specs=(
            pl.BlockSpec((req, length, cols), lambda i: (0, 0, i)),
            pl.BlockSpec((EXP_DEV * RANK, cols), lambda i: (0, i)),
            pl.BlockSpec((EXP_DEV * RANK, model), lambda i: (0, 0)),
        ),
        scratch_shapes=[pltpu.VMEM((rows, EXP_DEV * RANK), bf)],
        compiler_params=pltpu.CompilerParams(vmem_limit_bytes=32 << 20),
        name="finish",
    )(
        tab_all, pw.reshape(req, length, width), pair_in.reshape(req, width, ff),
        ret_in.reshape(rows, ff), ret_out.reshape(rows, model),
    )
    router_grad = jnp.sum(router[:, 0, :].reshape(req, top, RANK), axis=2)
    return (
        input_grad.reshape(tokens, ff),
        grad_in.reshape(EXP_DEV, RANK, ff),
        grad_out.reshape(EXP_DEV, RANK, model),
        router_grad,
    )


def solution(mesh):
    return jax.shard_map(
        body,
        mesh=mesh,
        in_specs=(
            P("adapter", "dp"),
            P("adapter", "dp"),
            P("adapter", None, "dp"),
            P("adapter", None, "dp"),
            P("adapter", None),
            P("adapter", None),
        ),
        out_specs=(
            P("adapter", "dp"),
            P("adapter", None, "dp"),
            P("adapter", None, "dp"),
            P("adapter", None),
        ),
        check_vma=False,
    )
```

time: 288 us -> 136 us (0.47)
  the two profiles are of different devices: /device:TPU:124 before, /device:TPU:0 now
where the time goes in v1:
time: 136 us; the launch traced here: 134 us
  Pallas kernels  126 us (93%)
  local copies, waits for them, and re-layouts  6.28 us (5%)
    pallas_call x1, Pallas kernels, body(): pl.pallas_call(exchange_kernel, out_shape=(jax.ShapeDtypeStruct((slots, R...  118 us
    pallas_call x1, Pallas kernels, body(): pl.pallas_call(finish_kernel, grid=(ff // cols,), out_shape=(jax.ShapeDty...  8.26 us
    unnamed x6, local copies, waits for them, and re-layouts  4.49 us

profile of v1, /device:TPU:0, one launch (start us, length us, event | category | flops | bytes accessed | tf_op | source)
XLA Modules:
  0.0 134.4 jit_solution(7748277569968717910)
XLA Ops:
  0.6 0.8 reshape.176
  1.4 0.2 convert_reduce_fusion
  1.6 0.1 select_reduce_fusion
  1.7 0.1 reshape.177
  1.8 0.8 broadcast_in_dim.35
  2.6 0.1 reshape.178.scale_ref
  2.7 0.0 copy-start.1
  2.7 1.2 copy-done.1
  3.9 0.0 copy-start.2
  3.9 1.2 copy-done.2
  5.1 118.2 %exchange.1 = (bf16[32,16,3584]{2,1,0:T(8,128)(2,1)}, bf16[32,16,1024]{2,1,0:T(8,128)(2,1)S(1)}, bf16[16,16,3584]{2,1,0:T(8,128)(2,1)S(1)}, bf16[8,64,128]{2,1,0...) custom-call(s32[16]{0:T(128)S(1)} %add_minimum_fusion.slot_of_pair, ...), custom_call_target="tpu_custom_call" | custom-call | tf_op jit(solution)/shard_map/exchange/pallas_call | solution.py:270
  123.4 0.1 reshape_squeeze.3
  123.4 0.7 reduce_sum.19
  124.1 0.0 copy-start
  124.1 2.0 %copy-done = bf16[32,16,3584]{2,1,0:T(8,128)(2,1)S(1)} copy-done((bf16[32,16,3584]{2,1,0:T(8,128)(2,1)S(1)}, bf16[32,16,3584]{2,1,0:T(8,128)(2,1)}, u32[]{:S(2)}) %copy-start) | copy-done | bytes 3670040
  126.1 8.3 %finish.1 = (f32[2,256,3584]{2,1,0:T(8,128)}, bf16[512,3584]{1,0:T(8,128)(2,1)}, bf16[512,1024]{1,0:T(8,128)(2,1)}) custom-call(s32[16,1,128]{2,1,0:T(1,128)S(1)} %get-tuple-element.13.tab, bf16[2,256,128]{2,1,0:T(8,128)(2,1)S(1)} %bitcast.14, bf16[2,128,3584]{2,1,0:T(8,128)(2,1)S(1)} %bitcast.11, bf16[512,3584]{1,0:T(8,128)(2,1)S(1)} %bitcast.10, ...), custom_call_target="tpu_custom_call" | custom-call | tf_op jit(solution)/shard_map/finish/pallas_call | solution.py:323
  (4 shorter events, 0.1 us)
Async XLA Ops:
  2.7 1.2 copy-start.1
  3.9 1.2 copy-start.2
  124.1 2.0 %copy-start = (bf16[32,16,3584]{2,1,0:T(8,128)(2,1)S(1)}, bf16[32,16,3584]{2,1,0:T(8,128)(2,1)}, u32[]{:S(2)}) copy-start(bf16[32,16,3584]{2,1,0:T(8,128)(2,1)} %get-tuple-element.16) | copy-start | bytes 11010052

commit v2 on v0

v2 whole, which is shorter than its diff:
```python
import jax
import jax.numpy as jnp
from jax import lax
from jax.experimental import pallas as pl
from jax.experimental.pallas import tpu as pltpu
from jax.sharding import PartitionSpec as P

MESH = pl.DeviceIdType.MESH
SIDE = 4
OWNERS = SIDE * SIDE
CAP = 2
RANK = 16
EXP_DEV = 32
DP = 8
HALF = DP // 2
LANES = 128
COLS = 512
FINAL = 256
PARTS = 2
ORDER = (
    (1, 1), (3, 3), (1, 3), (3, 1), (2, 0), (0, 2), (2, 2), (2, 1),
    (1, 2), (2, 3), (3, 2), (1, 0), (3, 0), (0, 1), (0, 3),
)
BF, F32, I32 = jnp.bfloat16, jnp.float32, jnp.int32


def rot(off):
    return off[0] * SIDE + off[1]


def exchange_kernel(
    ids, weights, fi_hbm, fo_hbm, act_hbm, cot_hbm,
    ig, gi, go, router,
    fi, fo, act, cot, send_in, send_out, got_in, got_out, pair_in, pair_out,
    term_in, term_out, back_in, back_out, ret_in, ret_out, place,
    tab_send, tab, tab_smem, inv, inv_smem, slot_of_pair,
    rs_send, rs_got, kept, ag, rp,
    load_sem, tab_sem, tab_ss, tab_rs, fo_ss, fo_rs, fi_ss, fi_rs,
    bi_ss, bi_rs, bo_ss, bo_rs, rs_ss, rs_rs, ag_ss, ag_rs, rp_ss, rp_rs,
):
    me = lax.axis_index("adapter")
    mx, mz = me // SIDE, me % SIDE
    dp = lax.axis_index("dp")
    top = ids.shape[1]
    pairs = 2 * top
    width = top * RANK
    length = act.shape[1]
    chunk = length // HALF

    def there(off):
        return {"adapter": ((mx + off[0]) % SIDE) * SIDE + (mz + off[1]) % SIDE}

    def back(off):
        return {"adapter": ((mx + SIDE - off[0]) % SIDE) * SIDE + (mz + SIDE - off[1]) % SIDE}

    def beside(d):
        return {"dp": (dp + d) % DP}

    def push(src, dst, ss, rs, dev):
        c = pltpu.make_async_remote_copy(
            src_ref=src, dst_ref=dst, send_sem=ss, recv_sem=rs, device_id=dev, device_id_type=MESH
        )
        c.start()
        return c

    bar = pltpu.get_barrier_semaphore()
    for off in ORDER:
        pl.semaphore_signal(bar, inc=1, device_id=there(off), device_id_type=MESH)
    for d in range(1, DP):
        pl.semaphore_signal(bar, inc=1, device_id=beside(d), device_id_type=MESH)

    loads = []
    for i, (src, dst) in enumerate(((fo_hbm, fo), (fi_hbm, fi), (cot_hbm, cot), (act_hbm, act))):
        loads.append(pltpu.make_async_copy(src, dst, load_sem.at[i]))
        loads[-1].start()

    row = lax.broadcasted_iota(I32, (OWNERS, LANES), 0)
    lane = lax.broadcasted_iota(I32, (OWNERS, LANES), 1)
    owner = []
    named = jnp.full((OWNERS, LANES), -1, I32)
    which = jnp.zeros((OWNERS, LANES), I32)
    for p in range(pairs):
        e = ids[p // top, p % top]
        o = lax.shift_right_logical(e, 5)
        nth = jnp.int32(0)
        for q in owner:
            nth = nth + jnp.where(q == o, 1, 0)
        owner.append(o)
        nth = jnp.minimum(nth, CAP - 1)
        turn = ((mx - lax.shift_right_logical(o, 2)) & 3) * SIDE + ((mz - o) & 3)
        slot_of_pair[p] = turn * CAP + nth
        hit = (row == turn) & (lane == nth)
        named = jnp.where(hit, e & (EXP_DEV - 1), named)
        which = jnp.where(hit, p, which)
    tab_send[...] = named
    inv[...] = which
    inv_copy = pltpu.make_async_copy(inv, inv_smem, tab_sem.at[1])
    inv_copy.start()

    pl.semaphore_wait(bar, len(ORDER) + DP - 1)
    tabs = []
    for i, off in enumerate(ORDER):
        at = pl.ds(rot(off), 1)
        tabs.append(push(tab_send.at[at], tab.at[at], tab_ss.at[i], tab_rs.at[i], back(off)))
    tab[0:1] = tab_send[0:1]
    for c in tabs:
        c.wait()
    tab_copy = pltpu.make_async_copy(tab, tab_smem, tab_sem.at[0])
    tab_copy.start()
    loads[0].wait()
    loads[1].wait()
    tab_copy.wait()

    def pick(src, dst, j, c):
        dst[j, c] = src[jnp.clip(tab_smem[j, c], 0, EXP_DEV - 1)]

    fos, fis = [], []
    for i, off in enumerate(ORDER):
        j = rot(off)
        for c in range(CAP):
            pick(fo, send_out, j, c)
        fos.append(push(send_out.at[j], got_out.at[j], fo_ss.at[i], fo_rs.at[i], there(off)))
    for c in range(CAP):
        pick(fo, got_out, 0, c)
    for c in range(CAP):
        for i, off in enumerate(ORDER):
            j = rot(off)
            pick(fi, send_in, j, c)
            n = c * len(ORDER) + i
            fis.append(push(send_in.at[j, c], got_in.at[j, c], fi_ss.at[n], fi_rs.at[n], there(off)))
    for c in range(CAP):
        pick(fi, got_in, 0, c)

    def project(step, rows, got, pair):
        for b in range(2):
            for k in range(top):
                p = b * top + k
                s = slot_of_pair[p]
                pair[p] = got[lax.shift_right_logical(s, 1), s & (CAP - 1)]
            part = lax.dot_general(
                rows[b], pair[b * top:(b + 1) * top].reshape(width, pair.shape[2]),
                (((1,), (1,)), ((), ())), preferred_element_type=F32,
            )
            for h in range(HALF):
                rs_send[step, b * HALF + h] = part[h * chunk:(h + 1) * chunk]

    def combine(step):
        cs = [
            push(rs_send.at[step, (dp + d) % DP], rs_got.at[step, d],
                 rs_ss.at[step, d], rs_rs.at[step, d], beside(d))
            for d in range(1, DP)
        ]
        total = rs_send[step, dp]
        for d in range(1, DP):
            cs[d - 1].wait()
            total = total + rs_got[step, d]
        return total

    group = lax.shift_right_logical(lax.broadcasted_iota(I32, (1, width), 1), 4)
    scale = jnp.zeros((1, width), F32)
    for k in range(top):
        scale = jnp.where(group == k, weights[dp // HALF, k], scale)

    def spread(step, total):
        ag[step, dp] = (total * scale).astype(BF)
        return [
            push(ag.at[step, dp], ag.at[step, dp], ag_ss.at[step, d], ag_rs.at[step, d], beside(d))
            for d in range(1, DP)
        ]

    def terms(step, rows, term):
        for b in range(2):
            w = ag[step, b * HALF:(b + 1) * HALF].reshape(length, width)
            for s in range(0, rows.shape[2], COLS):
                t = lax.dot_general(
                    w, rows[b, :, s:s + COLS], (((0,), (0,)), ((), ())), preferred_element_type=F32
                )
                term[b * top:(b + 1) * top, :, s:s + COLS] = t.astype(BF).reshape(top, RANK, COLS)

    loads[2].wait()
    loads[3].wait()
    inv_copy.wait()
    for c in fos:
        c.wait()
    project(0, cot, got_out, pair_out)
    pulled = combine(0)
    kept[...] = pulled
    for c in spread(0, pulled):
        c.wait()

    def give(term, out, ret, ss, rs, part, parts):
        n = term.shape[2] // parts
        at = pl.ds(part * n, n)
        cs = []
        for i, off in enumerate(ORDER):
            j = rot(off)
            for c in range(CAP):
                out[j, c, :, at] = term[inv_smem[j, c], :, at]
            k = part * len(ORDER) + i
            cs.append(push(out.at[j, :, :, at], ret.at[j, :, :, at], ss.at[k], rs.at[k], back(off)))
        for c in range(CAP):
            ret[0, c, :, at] = term[inv_smem[0, c], :, at]
        return cs

    terms(0, act, term_in)
    bis = [give(term_in, back_in, ret_in, bi_ss, bi_rs, part, PARTS) for part in range(PARTS)]

    for c in fis:
        c.wait()
    project(1, act, got_in, pair_in)
    projected = combine(1)
    ags = spread(1, projected)
    rp[dp] = jnp.broadcast_to(jnp.sum(projected * kept[...], axis=0, keepdims=True), rp.shape[1:])
    rps = [push(rp.at[dp], rp.at[dp], rp_ss.at[d], rp_rs.at[d], beside(d)) for d in range(1, DP)]
    for c in ags:
        c.wait()
    terms(1, cot, term_out)
    bos = give(term_out, back_out, ret_out, bo_ss, bo_rs, 0, 1)

    for b in range(2):
        w = ag[0, b * HALF:(b + 1) * HALF].reshape(length, width)
        f = pair_in.at[b * top:(b + 1) * top]
        for s in range(0, fi.shape[2], COLS):
            ig[b, :, s:s + COLS] = jnp.dot(
                w, f[:, :, s:s + COLS].reshape(width, COLS), preferred_element_type=F32
            )
    for c in rps:
        c.wait()
    sums = jnp.concatenate(
        [jnp.sum(rp[b * HALF:(b + 1) * HALF], axis=0)[0:1] for b in range(2)]
        + [jnp.zeros((6, width), F32)], axis=0,
    )
    fold = jnp.where(
        lax.shift_right_logical(lax.broadcasted_iota(I32, (width, LANES), 0), 4)
        == lax.broadcasted_iota(I32, (width, LANES), 1), 1.0, 0.0,
    )
    router[...] = jnp.dot(
        sums, fold, precision=lax.Precision.HIGHEST, preferred_element_type=F32
    )[0:2, 0:top]

    total_rows = EXP_DEV * RANK
    slots = OWNERS * CAP
    spot = lax.broadcasted_iota(I32, (1, slots * RANK), 1)
    target = jnp.full((1, slots * RANK), -1, I32)
    for s in range(slots):
        e = tab_smem[s // CAP, s % CAP]
        target = jnp.where(lax.shift_right_logical(spot, 4) == s, e * RANK + (spot & (RANK - 1)), target)
    for r in range(0, total_rows, LANES):
        at = lax.broadcasted_iota(I32, (LANES, slots * RANK), 0) + r
        place[r:r + LANES, :] = jnp.where(at == target, 1.0, 0.0).astype(BF)

    def settle(ret, grad, start, stop):
        for s in range(start, stop, FINAL):
            total = jnp.dot(
                place[...], ret[:, :, :, s:s + FINAL].reshape(slots * RANK, FINAL), preferred_element_type=F32
            )
            grad[:, :, s:s + FINAL] = total.astype(BF).reshape(EXP_DEV, RANK, FINAL)

    ff = fi.shape[2]
    for part in range(PARTS):
        for c in bis[part]:
            c.wait()
        settle(ret_in, gi, part * ff // PARTS, (part + 1) * ff // PARTS)
    for c in bos:
        c.wait()
    settle(ret_out, go, 0, fo.shape[2])


def body(activations, cotangent, factor_in, factor_out, adapter_ids, router_weights):
    req, top = adapter_ids.shape
    tokens, ff = activations.shape
    model = cotangent.shape[1]
    length = tokens // req
    pairs = req * top
    chunk = tokens // DP
    width = top * RANK
    hbm = pl.BlockSpec(memory_space=pltpu.HBM)
    smem = pl.BlockSpec(memory_space=pltpu.SMEM)
    vmem = pl.BlockSpec(memory_space=pltpu.VMEM)
    dma = pltpu.SemaphoreType.DMA
    far = OWNERS - 1

    def slots(n):
        return pltpu.VMEM((OWNERS, CAP, RANK, n), BF)

    def by_pair(n):
        return pltpu.VMEM((pairs, RANK, n), BF)

    input_grad, grad_in, grad_out, router_grad = pl.pallas_call(
        exchange_kernel,
        out_shape=(
            pltpu.VMEM((req, length, ff), F32),
            pltpu.VMEM((EXP_DEV, RANK, ff), BF),
            pltpu.VMEM((EXP_DEV, RANK, model), BF),
            pltpu.VMEM((req, top), F32),
        ),
        in_specs=[smem, smem, hbm, hbm, hbm, hbm],
        out_specs=(vmem, vmem, vmem, vmem),
        scratch_shapes=[
            pltpu.VMEM((EXP_DEV, RANK, ff), BF),
            pltpu.VMEM((EXP_DEV, RANK, model), BF),
            pltpu.VMEM((req, length, ff), BF),
            pltpu.VMEM((req, length, model), BF),
            slots(ff), slots(model), slots(ff), slots(model),
            by_pair(ff), by_pair(model), by_pair(ff), by_pair(model),
            slots(ff), slots(model), slots(ff), slots(model),
            pltpu.VMEM((EXP_DEV * RANK, OWNERS * CAP * RANK), BF),
            pltpu.VMEM((OWNERS, LANES), I32),
            pltpu.VMEM((OWNERS, LANES), I32),
            pltpu.SMEM((OWNERS, LANES), I32),
            pltpu.VMEM((OWNERS, LANES), I32),
            pltpu.SMEM((OWNERS, LANES), I32),
            pltpu.SMEM((pairs,), I32),
            pltpu.VMEM((2, DP, chunk, width), F32),
            pltpu.VMEM((2, DP, chunk, width), F32),
            pltpu.VMEM((chunk, width), F32),
            pltpu.VMEM((2, DP, chunk, width), BF),
            pltpu.VMEM((DP, 8, width), F32),
            dma((4,)), dma((2,)),
            dma((far,)), dma((far,)),
            dma((far,)), dma((far,)),
            dma((CAP * far,)), dma((CAP * far,)),
            dma((PARTS * far,)), dma((PARTS * far,)),
            dma((far,)), dma((far,)),
            dma((2, DP)), dma((2, DP)), dma((2, DP)), dma((2, DP)), dma((DP,)), dma((DP,)),
        ],
        compiler_params=pltpu.CompilerParams(
            collective_id=0, has_side_effects=True, vmem_limit_bytes=44 << 20
        ),
        name="exchange",
    )(
        adapter_ids,
        router_weights,
        *(
            pltpu.with_memory_space_constraint(x, pltpu.HBM)
            for x in (
                factor_in, factor_out,
                activations.reshape(req, length, ff), cotangent.reshape(req, length, model),
            )
        ),
    )
    return input_grad.reshape(tokens, ff), grad_in, grad_out, router_grad


def solution(mesh):
    return jax.shard_map(
        body,
        mesh=mesh,
        in_specs=(
            P("adapter", "dp"),
            P("adapter", "dp"),
            P("adapter", None, "dp"),
            P("adapter", None, "dp"),
            P("adapter", None),
            P("adapter", None),
        ),
        out_specs=(
            P("adapter", "dp"),
            P("adapter", None, "dp"),
            P("adapter", None, "dp"),
            P("adapter", None),
        ),
        check_vma=False,
    )
```

time: 288 us -> 127 us (0.44)
  the two profiles are of different devices: /device:TPU:124 before, /device:TPU:0 now
where the time goes in v2:
time: 127 us; the launch traced here: 126 us
  Pallas kernels  119 us (94%)
  local copies, waits for them, and re-layouts  6.42 us (5%)
    pallas_call x1, Pallas kernels, body(): pl.pallas_call(exchange_kernel, out_shape=(pltpu.VMEM((req, length, ff),...  119 us
    unnamed x4, local copies, waits for them, and re-layouts  6.42 us

profile of v2, /device:TPU:0, one launch (start us, length us, event | category | flops | bytes accessed | tf_op | source)
XLA Modules:
  0.0 126.1 jit_solution(11155307411736184817)
XLA Ops:
  0.6 119.0 %exchange.1 = (f32[2,256,3584]{2,1,0:T(8,128)S(1)}, bf16[32,16,3584]{2,1,0:T(8,128)(2,1)S(1)}, bf16[32,16,1024]{2,1,0:T(8,128)(2,1)S(1)}, f32[2,8]{1,0:T(2,128)S(1)}) custom-call(s32[2,8]{1,0:T(2,128)} %ids.1, f32[2,8]{1,0:T(2,128)} %weights.1, bf16[32,16,3584]{2,1,0:T(8,128)(2,1)} %fi_hbm.1, bf16[32,16,1024]{2,1,0:T(8,128)(2,1)} %fo_hbm.1, ...), custom_call_target="tpu_custom_call" | custom-call | tf_op jit(solution)/shard_map/exchange/pallas_call | solution.py:289
  119.7 3.1 %copy.14 = f32[512,3584]{1,0:T(8,128)} copy(f32[512,3584]{1,0:T(8,128)S(1)} %bitcast.3) | data formatting | bytes 14680064
  122.7 0.6 copy.17
  123.3 1.0 copy.16
  124.2 1.8 %copy.15 = bf16[32,16,3584]{2,1,0:T(8,128)(2,1)} copy(bf16[32,16,3584]{2,1,0:T(8,128)(2,1)S(1)} %get-tuple-element.13) | data formatting | bytes 7340032

commit v3 on v2

--- a/solution.py
+++ b/solution.py
@@ -17,6 +17,7 @@
 COLS = 512
 FINAL = 256
 PARTS = 2
+SPLIT = 4
 ORDER = (
     (1, 1), (3, 3), (1, 3), (3, 1), (2, 0), (0, 2), (2, 2), (2, 1),
     (1, 2), (2, 3), (3, 2), (1, 0), (3, 0), (0, 1), (0, 3),
@@ -249,21 +250,37 @@
         at = lax.broadcasted_iota(I32, (LANES, slots * RANK), 0) + r
         place[r:r + LANES, :] = jnp.where(at == target, 1.0, 0.0).astype(BF)
 
-    def settle(ret, grad, start, stop):
-        for s in range(start, stop, FINAL):
+    def settle(ret, grad, start, stop, step):
+        for s in range(start, stop, step):
             total = jnp.dot(
-                place[...], ret[:, :, :, s:s + FINAL].reshape(slots * RANK, FINAL), preferred_element_type=F32
+                place[...], ret[:, :, :, s:s + step].reshape(slots * RANK, step), preferred_element_type=F32
             )
-            grad[:, :, s:s + FINAL] = total.astype(BF).reshape(EXP_DEV, RANK, FINAL)
+            grad[:, :, s:s + step] = total.astype(BF).reshape(EXP_DEV, RANK, step)
 
     ff = fi.shape[2]
     for part in range(PARTS):
         for c in bis[part]:
             c.wait()
-        settle(ret_in, gi, part * ff // PARTS, (part + 1) * ff // PARTS)
+        settle(ret_in, gi, part * ff // PARTS, (part + 1) * ff // PARTS, FINAL)
     for c in bos:
         c.wait()
-    settle(ret_out, go, 0, fo.shape[2])
+    settle(ret_out, go, 0, fo.shape[2], 256)
+
+
+def store_kernel(*refs):
+    n = len(refs) // 2
+    srcs, dsts, sem = refs[:n], refs[n:2 * n], refs[-1]
+    copies = []
+    for src, dst in zip(srcs, dsts):
+        parts = SPLIT if src.shape[0] % SPLIT == 0 else 1
+        step = src.shape[0] // parts
+        for p in range(parts):
+            at = pl.ds(p * step, step)
+            copies.append(pltpu.make_async_copy(src.at[at], dst.at[at], sem.at[len(copies)]))
+    for c in copies:
+        c.start()
+    for c in copies:
+        c.wait()
 
 
 def body(activations, cotangent, factor_in, factor_out, adapter_ids, router_weights):
@@ -286,7 +303,7 @@
     def by_pair(n):
         return pltpu.VMEM((pairs, RANK, n), BF)
 
-    input_grad, grad_in, grad_out, router_grad = pl.pallas_call(
+    results = pl.pallas_call(
         exchange_kernel,
         out_shape=(
             pltpu.VMEM((req, length, ff), F32),
@@ -339,6 +356,15 @@
             )
         ),
     )
+    input_grad, grad_in, grad_out, router_grad = pl.pallas_call(
+        store_kernel,
+        out_shape=tuple(jax.ShapeDtypeStruct(r.shape, r.dtype) for r in results),
+        in_specs=[vmem] * 4,
+        out_specs=(hbm,) * 4,
+        scratch_shapes=[dma((4 * SPLIT,))],
+        compiler_params=pltpu.CompilerParams(vmem_limit_bytes=1 << 20),
+        name="store",
+    )(*(pltpu.with_memory_space_constraint(r, pltpu.VMEM) for r in results))
     return input_grad.reshape(tokens, ff), grad_in, grad_out, router_grad
 
 

time: 127 us -> 125 us (0.984)
  local copies, waits for them, and re-layouts: 6.42 us -> 0 us
  Pallas kernels: 119 us -> 124 us
    unnamed x4 -> x0, local copies, waits for them, and re-layouts: 6.42 us -> none
    pallas_call x0 -> x1, Pallas kernels: none -> 4.6 us  [body(): pl.pallas_call(store_kernel, out_shape=tuple((jax.ShapeDtypeStruct(r.shap...]
where the time goes in v3:
time: 125 us; the launch traced here: 124 us
  Pallas kernels  124 us (99%)
    pallas_call x1, Pallas kernels, body(): pl.pallas_call(exchange_kernel, out_shape=(pltpu.VMEM((req, length, ff),...  119 us
    pallas_call x1, Pallas kernels, body(): pl.pallas_call(store_kernel, out_shape=tuple((jax.ShapeDtypeStruct(r.shap...  4.6 us

profile of v3, /device:TPU:0, one launch (start us, length us, event | category | flops | bytes accessed | tf_op | source)
XLA Modules:
  0.0 124.3 jit_solution(16026079171960633020)
XLA Ops:
  0.6 119.0 %exchange.1 = (f32[2,256,3584]{2,1,0:T(8,128)S(1)}, bf16[32,16,3584]{2,1,0:T(8,128)(2,1)S(1)}, bf16[32,16,1024]{2,1,0:T(8,128)(2,1)S(1)}, f32[2,8]{1,0:T(2,128)S(1)}) custom-call(s32[2,8]{1,0:T(2,128)} %ids.1, f32[2,8]{1,0:T(2,128)} %weights.1, bf16[32,16,3584]{2,1,0:T(8,128)(2,1)} %fi_hbm.1, bf16[32,16,1024]{2,1,0:T(8,128)(2,1)} %fo_hbm.1, ...), custom_call_target="tpu_custom_call" | custom-call | tf_op jit(solution)/shard_map/exchange/pallas_call | solution.py:306
  119.7 4.6 %store.1 = (f32[2,256,3584]{2,1,0:T(8,128)}, bf16[32,16,3584]{2,1,0:T(8,128)(2,1)}, bf16[32,16,1024]{2,1,0:T(8,128)(2,1)}, f32[2,8]{1,0:T(2,128)}) custom-call(f32[2,256,3584]{2,1,0:T(8,128)S(1)} %get-tuple-element.12.refs_0_, bf16[32,16,3584]{2,1,0:T(8,128)(2,1)S(1)} %get-tuple-element.13.refs_1_, bf16[32,16,1024]{2,1,0:T(8,128)(2,1)S(1)} %get-tuple-element.14.refs_2_, ...), custom_call_target="tpu_custom_call" | custom-call | tf_op jit(solution)/shard_map/store/pallas_call | solution.py:359

commit v4 on v3

--- a/solution.py
+++ b/solution.py
@@ -17,11 +17,12 @@
 COLS = 512
 FINAL = 256
 PARTS = 2
-SPLIT = 4
-ORDER = (
-    (1, 1), (3, 3), (1, 3), (3, 1), (2, 0), (0, 2), (2, 2), (2, 1),
-    (1, 2), (2, 3), (3, 2), (1, 0), (3, 0), (0, 1), (0, 3),
-)
+SPLIT = 1
+ORDER = ((2, 0), (0, 2), (1, 0), (3, 0), (0, 1), (0, 3), (1, 1), (3, 3), (1, 3), (3, 1), (2, 1), (2, 3), (1, 2), (3, 2), (2, 2))
+ORDER_FO = ((2, 0), (0, 2), (1, 0), (3, 0), (0, 1), (0, 3), (1, 1), (3, 3), (1, 3), (3, 1), (2, 1), (2, 3), (1, 2), (3, 2), (2, 2))
+ORDER_FI = ((2, 0), (0, 2), (1, 0), (3, 0), (0, 1), (0, 3), (1, 1), (3, 3), (1, 3), (3, 1), (2, 1), (2, 3), (1, 2), (3, 2), (2, 2))
+ORDER_BI = ((2, 0), (0, 2), (1, 0), (3, 0), (0, 1), (0, 3), (1, 1), (3, 3), (1, 3), (3, 1), (2, 1), (2, 3), (1, 2), (3, 2), (2, 2))
+ORDER_BO = ((2, 2), (2, 1), (2, 3), (1, 2), (3, 2), (1, 1), (3, 3), (1, 3), (3, 1), (2, 0), (0, 2), (1, 0), (3, 0), (0, 1), (0, 3))
 BF, F32, I32 = jnp.bfloat16, jnp.float32, jnp.int32
 
 
@@ -30,11 +31,11 @@
 
 
 def exchange_kernel(
-    ids, weights, fi_hbm, fo_hbm, act_hbm, cot_hbm,
+    ids_hbm, weights_hbm, fi_hbm, fo_hbm, act_hbm, cot_hbm,
     ig, gi, go, router,
     fi, fo, act, cot, send_in, send_out, got_in, got_out, pair_in, pair_out,
     term_in, term_out, back_in, back_out, ret_in, ret_out, place,
-    tab_send, tab, tab_smem, inv, inv_smem, slot_of_pair,
+    ids, weights, tab_send, tab_got, tab, inv, inv_smem, slot_of_pair,
     rs_send, rs_got, kept, ag, rp,
     load_sem, tab_sem, tab_ss, tab_rs, fo_ss, fo_rs, fi_ss, fi_rs,
     bi_ss, bi_rs, bo_ss, bo_rs, rs_ss, rs_rs, ag_ss, ag_rs, rp_ss, rp_rs,
@@ -64,73 +65,88 @@
         c.start()
         return c
 
+    loads = []
+    for i, (src, dst) in enumerate(((fo_hbm, fo), (fi_hbm, fi), (cot_hbm, cot), (act_hbm, act))):
+        loads.append(pltpu.make_async_copy(src, dst, load_sem.at[i]))
+    id_copies = [
+        pltpu.make_async_copy(ids_hbm, ids, tab_sem.at[2]),
+        pltpu.make_async_copy(weights_hbm, weights, tab_sem.at[3]),
+    ]
+    for c in id_copies:
+        c.start()
     bar = pltpu.get_barrier_semaphore()
     for off in ORDER:
         pl.semaphore_signal(bar, inc=1, device_id=there(off), device_id_type=MESH)
     for d in range(1, DP):
         pl.semaphore_signal(bar, inc=1, device_id=beside(d), device_id_type=MESH)
-
-    loads = []
-    for i, (src, dst) in enumerate(((fo_hbm, fo), (fi_hbm, fi), (cot_hbm, cot), (act_hbm, act))):
-        loads.append(pltpu.make_async_copy(src, dst, load_sem.at[i]))
-        loads[-1].start()
+    for c in loads:
+        c.start()
+
+    def turn_of(p):
+        o = lax.shift_right_logical(ids[p // top, p % top], 5)
+        return ((mx - lax.shift_right_logical(o, 2)) & 3) * SIDE + ((mz - o) & 3)
 
     row = lax.broadcasted_iota(I32, (OWNERS, LANES), 0)
     lane = lax.broadcasted_iota(I32, (OWNERS, LANES), 1)
-    owner = []
     named = jnp.full((OWNERS, LANES), -1, I32)
     which = jnp.zeros((OWNERS, LANES), I32)
+    held = jnp.zeros((OWNERS, LANES), I32)
+    id_copies[0].wait()
     for p in range(pairs):
-        e = ids[p // top, p % top]
-        o = lax.shift_right_logical(e, 5)
-        nth = jnp.int32(0)
-        for q in owner:
-            nth = nth + jnp.where(q == o, 1, 0)
-        owner.append(o)
-        nth = jnp.minimum(nth, CAP - 1)
-        turn = ((mx - lax.shift_right_logical(o, 2)) & 3) * SIDE + ((mz - o) & 3)
-        slot_of_pair[p] = turn * CAP + nth
-        hit = (row == turn) & (lane == nth)
-        named = jnp.where(hit, e & (EXP_DEV - 1), named)
+        mine = row == turn_of(p)
+        hit = mine & (lane == held)
+        named = jnp.where(hit, ids[p // top, p % top] & (EXP_DEV - 1), named)
         which = jnp.where(hit, p, which)
+        held = jnp.where(mine, held + 1, held)
     tab_send[...] = named
-    inv[...] = which
-    inv_copy = pltpu.make_async_copy(inv, inv_smem, tab_sem.at[1])
-    inv_copy.start()
 
     pl.semaphore_wait(bar, len(ORDER) + DP - 1)
     tabs = []
     for i, off in enumerate(ORDER):
         at = pl.ds(rot(off), 1)
-        tabs.append(push(tab_send.at[at], tab.at[at], tab_ss.at[i], tab_rs.at[i], back(off)))
-    tab[0:1] = tab_send[0:1]
+        tabs.append(push(tab_send.at[at], tab_got.at[at], tab_ss.at[i], tab_rs.at[i], back(off)))
+    tab_got[0:1] = named[0:1]
+    inv[...] = which
+    inv_copy = pltpu.make_async_copy(inv, inv_smem, tab_sem.at[1])
+    inv_copy.start()
+
+    def pick(src, dst, j, c):
+        dst[j, c] = src[jnp.clip(tab[j, c], 0, EXP_DEV - 1)]
+
+    fos, fis = [], []
+    loads[0].wait()
     for c in tabs:
-        c.wait()
-    tab_copy = pltpu.make_async_copy(tab, tab_smem, tab_sem.at[0])
+        c.wait_recv()
+    tab_copy = pltpu.make_async_copy(tab_got, tab, tab_sem.at[0])
     tab_copy.start()
-    loads[0].wait()
-    loads[1].wait()
     tab_copy.wait()
-
-    def pick(src, dst, j, c):
-        dst[j, c] = src[jnp.clip(tab_smem[j, c], 0, EXP_DEV - 1)]
-
-    fos, fis = [], []
-    for i, off in enumerate(ORDER):
+    for i, off in enumerate(ORDER_FO):
         j = rot(off)
         for c in range(CAP):
             pick(fo, send_out, j, c)
         fos.append(push(send_out.at[j], got_out.at[j], fo_ss.at[i], fo_rs.at[i], there(off)))
     for c in range(CAP):
         pick(fo, got_out, 0, c)
+    loads[1].wait()
     for c in range(CAP):
-        for i, off in enumerate(ORDER):
+        for i, off in enumerate(ORDER_FI):
             j = rot(off)
             pick(fi, send_in, j, c)
             n = c * len(ORDER) + i
             fis.append(push(send_in.at[j, c], got_in.at[j, c], fi_ss.at[n], fi_rs.at[n], there(off)))
     for c in range(CAP):
         pick(fi, got_in, 0, c)
+    for c in tabs:
+        c.wait_send()
+    turns = []
+    for p in range(pairs):
+        nth = jnp.int32(0)
+        t = turn_of(p)
+        for q in turns:
+            nth = nth + jnp.where(q == t, 1, 0)
+        turns.append(t)
+        slot_of_pair[p] = t * CAP + jnp.minimum(nth, CAP - 1)
+    id_copies[1].wait()
 
     def project(step, rows, got, pair):
         for b in range(2):
@@ -189,11 +205,11 @@
     for c in spread(0, pulled):
         c.wait()
 
-    def give(term, out, ret, ss, rs, part, parts):
+    def give(order, term, out, ret, ss, rs, part, parts):
         n = term.shape[2] // parts
         at = pl.ds(part * n, n)
         cs = []
-        for i, off in enumerate(ORDER):
+        for i, off in enumerate(order):
             j = rot(off)
             for c in range(CAP):
                 out[j, c, :, at] = term[inv_smem[j, c], :, at]
@@ -204,7 +220,7 @@
         return cs
 
     terms(0, act, term_in)
-    bis = [give(term_in, back_in, ret_in, bi_ss, bi_rs, part, PARTS) for part in range(PARTS)]
+    bis = [give(ORDER_BI, term_in, back_in, ret_in, bi_ss, bi_rs, part, PARTS) for part in range(PARTS)]
 
     for c in fis:
         c.wait()
@@ -216,7 +232,7 @@
     for c in ags:
         c.wait()
     terms(1, cot, term_out)
-    bos = give(term_out, back_out, ret_out, bo_ss, bo_rs, 0, 1)
+    bos = give(ORDER_BO, term_out, back_out, ret_out, bo_ss, bo_rs, 0, 1)
 
     for b in range(2):
         w = ag[0, b * HALF:(b + 1) * HALF].reshape(length, width)
@@ -244,7 +260,7 @@
     spot = lax.broadcasted_iota(I32, (1, slots * RANK), 1)
     target = jnp.full((1, slots * RANK), -1, I32)
     for s in range(slots):
-        e = tab_smem[s // CAP, s % CAP]
+        e = tab[s // CAP, s % CAP]
         target = jnp.where(lax.shift_right_logical(spot, 4) == s, e * RANK + (spot & (RANK - 1)), target)
     for r in range(0, total_rows, LANES):
         at = lax.broadcasted_iota(I32, (LANES, slots * RANK), 0) + r
@@ -292,7 +308,6 @@
     chunk = tokens // DP
     width = top * RANK
     hbm = pl.BlockSpec(memory_space=pltpu.HBM)
-    smem = pl.BlockSpec(memory_space=pltpu.SMEM)
     vmem = pl.BlockSpec(memory_space=pltpu.VMEM)
     dma = pltpu.SemaphoreType.DMA
     far = OWNERS - 1
@@ -311,7 +326,7 @@
             pltpu.VMEM((EXP_DEV, RANK, model), BF),
             pltpu.VMEM((req, top), F32),
         ),
-        in_specs=[smem, smem, hbm, hbm, hbm, hbm],
+        in_specs=[hbm] * 6,
         out_specs=(vmem, vmem, vmem, vmem),
         scratch_shapes=[
             pltpu.VMEM((EXP_DEV, RANK, ff), BF),
@@ -322,6 +337,8 @@
             by_pair(ff), by_pair(model), by_pair(ff), by_pair(model),
             slots(ff), slots(model), slots(ff), slots(model),
             pltpu.VMEM((EXP_DEV * RANK, OWNERS * CAP * RANK), BF),
+            pltpu.SMEM((req, top), I32),
+            pltpu.SMEM((req, top), F32),
             pltpu.VMEM((OWNERS, LANES), I32),
             pltpu.VMEM((OWNERS, LANES), I32),
             pltpu.SMEM((OWNERS, LANES), I32),
@@ -333,7 +350,7 @@
             pltpu.VMEM((chunk, width), F32),
             pltpu.VMEM((2, DP, chunk, width), BF),
             pltpu.VMEM((DP, 8, width), F32),
-            dma((4,)), dma((2,)),
+            dma((4,)), dma((4,)),
             dma((far,)), dma((far,)),
             dma((far,)), dma((far,)),
             dma((CAP * far,)), dma((CAP * far,)),
@@ -346,12 +363,10 @@
         ),
         name="exchange",
     )(
-        adapter_ids,
-        router_weights,
         *(
             pltpu.with_memory_space_constraint(x, pltpu.HBM)
             for x in (
-                factor_in, factor_out,
+                adapter_ids, router_weights, factor_in, factor_out,
                 activations.reshape(req, length, ff), cotangent.reshape(req, length, model),
             )
         ),

time: 125 us -> 125 us (level)
  no operation moved by 1% of the time
where the time goes in v4:
time: 125 us
  Pallas kernels  124 us (99%)
    pallas_call x1, Pallas kernels, body(): pl.pallas_call(exchange_kernel, out_shape=(pltpu.VMEM((req, length, ff),...  120 us
    pallas_call x1, Pallas kernels, body(): pl.pallas_call(store_kernel, out_shape=tuple((jax.ShapeDtypeStruct(r.shap...  4.53 us

profile of v4, /device:TPU:0, one launch (start us, length us, event | category | flops | bytes accessed | tf_op | source)
XLA Modules:
  0.0 125.0 jit_solution(3913947165790355985)
XLA Ops:
  0.6 119.8 %exchange.1 = (f32[2,256,3584]{2,1,0:T(8,128)S(1)}, bf16[32,16,3584]{2,1,0:T(8,128)(2,1)S(1)}, bf16[32,16,1024]{2,1,0:T(8,128)(2,1)S(1)}, f32[2,8]{1,0:T(2,128)S(1)}) custom-call(s32[2,8]{1,0:T(2,128)} %ids_hbm.1, f32[2,8]{1,0:T(2,128)} %weights_hbm.1, bf16[32,16,3584]{2,1,0:T(8,128)(2,1)} %fi_hbm.1, bf16[32,16,1024]{2,1,0:T(8,128)(2,1)} %fo_hbm.1, ...), custom_call_target="tpu_custom_call" | custom-call | tf_op jit(solution)/shard_map/exchange/pallas_call | solution.py:321
  120.5 4.5 %store.1 = (f32[2,256,3584]{2,1,0:T(8,128)}, bf16[32,16,3584]{2,1,0:T(8,128)(2,1)}, bf16[32,16,1024]{2,1,0:T(8,128)(2,1)}, f32[2,8]{1,0:T(2,128)}) custom-call(f32[2,256,3584]{2,1,0:T(8,128)S(1)} %get-tuple-element.12.refs_0_, bf16[32,16,3584]{2,1,0:T(8,128)(2,1)S(1)} %get-tuple-element.13.refs_1_, bf16[32,16,1024]{2,1,0:T(8,128)(2,1)S(1)} %get-tuple-element.14.refs_2_, ...), custom_call_target="tpu_custom_call" | custom-call | tf_op jit(solution)/shard_map/store/pallas_call | solution.py:374

commit v5 on v4

--- a/solution.py
+++ b/solution.py
@@ -110,32 +110,32 @@
     inv_copy = pltpu.make_async_copy(inv, inv_smem, tab_sem.at[1])
     inv_copy.start()
 
-    def pick(src, dst, j, c):
-        dst[j, c] = src[jnp.clip(tab[j, c], 0, EXP_DEV - 1)]
+    def pick(src, dst, j, c, named_here):
+        dst[j, c] = src[jnp.clip(named_here, 0, EXP_DEV - 1)]
 
     fos, fis = [], []
     loads[0].wait()
-    for c in tabs:
-        c.wait_recv()
+    for i, off in enumerate(ORDER_FO):
+        j = rot(off)
+        tabs[ORDER.index(off)].wait_recv()
+        here = tab_got[j:j + 1]
+        for c in range(CAP):
+            pick(fo, send_out, j, c, here[0, c])
+        fos.append(push(send_out.at[j], got_out.at[j], fo_ss.at[i], fo_rs.at[i], there(off)))
     tab_copy = pltpu.make_async_copy(tab_got, tab, tab_sem.at[0])
     tab_copy.start()
     tab_copy.wait()
-    for i, off in enumerate(ORDER_FO):
-        j = rot(off)
-        for c in range(CAP):
-            pick(fo, send_out, j, c)
-        fos.append(push(send_out.at[j], got_out.at[j], fo_ss.at[i], fo_rs.at[i], there(off)))
     for c in range(CAP):
-        pick(fo, got_out, 0, c)
+        pick(fo, got_out, 0, c, tab[0, c])
     loads[1].wait()
     for c in range(CAP):
         for i, off in enumerate(ORDER_FI):
             j = rot(off)
-            pick(fi, send_in, j, c)
+            pick(fi, send_in, j, c, tab[j, c])
             n = c * len(ORDER) + i
             fis.append(push(send_in.at[j, c], got_in.at[j, c], fi_ss.at[n], fi_rs.at[n], there(off)))
     for c in range(CAP):
-        pick(fi, got_in, 0, c)
+        pick(fi, got_in, 0, c, tab[0, c])
     for c in tabs:
         c.wait_send()
     turns = []

time: 125 us -> 123 us (0.984)
  Pallas kernels: 124 us -> 122 us
    pallas_call x1, Pallas kernels: 120 us -> 118 us  [body(): pl.pallas_call(exchange_kernel, out_shape=(pltpu.VMEM((req, length, ff),...]
where the time goes in v5:
time: 123 us
  Pallas kernels  122 us (99%)
    pallas_call x1, Pallas kernels, body(): pl.pallas_call(exchange_kernel, out_shape=(pltpu.VMEM((req, length, ff),...  118 us
    pallas_call x1, Pallas kernels, body(): pl.pallas_call(store_kernel, out_shape=tuple((jax.ShapeDtypeStruct(r.shap...  4.53 us

profile of v5, /device:TPU:0, one launch (start us, length us, event | category | flops | bytes accessed | tf_op | source)
XLA Modules:
  0.0 123.0 jit_solution(11034697213838803128)
XLA Ops:
  0.6 117.8 %exchange.1 = (f32[2,256,3584]{2,1,0:T(8,128)S(1)}, bf16[32,16,3584]{2,1,0:T(8,128)(2,1)S(1)}, bf16[32,16,1024]{2,1,0:T(8,128)(2,1)S(1)}, f32[2,8]{1,0:T(2,128)S(1)}) custom-call(s32[2,8]{1,0:T(2,128)} %ids_hbm.1, f32[2,8]{1,0:T(2,128)} %weights_hbm.1, bf16[32,16,3584]{2,1,0:T(8,128)(2,1)} %fi_hbm.1, bf16[32,16,1024]{2,1,0:T(8,128)(2,1)} %fo_hbm.1, ...), custom_call_target="tpu_custom_call" | custom-call | tf_op jit(solution)/shard_map/exchange/pallas_call | solution.py:321
  118.5 4.5 %store.1 = (f32[2,256,3584]{2,1,0:T(8,128)}, bf16[32,16,3584]{2,1,0:T(8,128)(2,1)}, bf16[32,16,1024]{2,1,0:T(8,128)(2,1)}, f32[2,8]{1,0:T(2,128)}) custom-call(f32[2,256,3584]{2,1,0:T(8,128)S(1)} %get-tuple-element.12.refs_0_, bf16[32,16,3584]{2,1,0:T(8,128)(2,1)S(1)} %get-tuple-element.13.refs_1_, bf16[32,16,1024]{2,1,0:T(8,128)(2,1)S(1)} %get-tuple-element.14.refs_2_, ...), custom_call_target="tpu_custom_call" | custom-call | tf_op jit(solution)/shard_map/store/pallas_call | solution.py:374

commit v6 on v5

--- a/solution.py
+++ b/solution.py
@@ -88,14 +88,17 @@
 
     row = lax.broadcasted_iota(I32, (OWNERS, LANES), 0)
     lane = lax.broadcasted_iota(I32, (OWNERS, LANES), 1)
-    named = jnp.full((OWNERS, LANES), -1, I32)
+    both = lane == CAP
+    named = jnp.where(both, 0, -1)
     which = jnp.zeros((OWNERS, LANES), I32)
     held = jnp.zeros((OWNERS, LANES), I32)
     id_copies[0].wait()
     for p in range(pairs):
         mine = row == turn_of(p)
         hit = mine & (lane == held)
-        named = jnp.where(hit, ids[p // top, p % top] & (EXP_DEV - 1), named)
+        e = ids[p // top, p % top] & (EXP_DEV - 1)
+        named = jnp.where(hit, e, named)
+        named = jnp.where(mine & both, named + jnp.where(held == 0, e, e * EXP_DEV), named)
         which = jnp.where(hit, p, which)
         held = jnp.where(mine, held + 1, held)
     tab_send[...] = named
@@ -119,8 +122,9 @@
         j = rot(off)
         tabs[ORDER.index(off)].wait_recv()
         here = tab_got[j:j + 1]
-        for c in range(CAP):
-            pick(fo, send_out, j, c, here[0, c])
+        pair = here[0, CAP]
+        pick(fo, send_out, j, 0, pair & (EXP_DEV - 1))
+        pick(fo, send_out, j, 1, lax.shift_right_logical(pair, 5) & (EXP_DEV - 1))
         fos.append(push(send_out.at[j], got_out.at[j], fo_ss.at[i], fo_rs.at[i], there(off)))
     tab_copy = pltpu.make_async_copy(tab_got, tab, tab_sem.at[0])
     tab_copy.start()

time: 123 us -> 123 us (level)
  no operation moved by 1% of the time
where the time goes in v6:
time: 123 us
  Pallas kernels  122 us (99%)
    pallas_call x1, Pallas kernels, body(): pl.pallas_call(exchange_kernel, out_shape=(pltpu.VMEM((req, length, ff),...  118 us
    pallas_call x1, Pallas kernels, body(): pl.pallas_call(store_kernel, out_shape=tuple((jax.ShapeDtypeStruct(r.shap...  4.53 us

profile of v6, /device:TPU:0, one launch (start us, length us, event | category | flops | bytes accessed | tf_op | source)
XLA Modules:
  0.0 123.0 jit_solution(2944153028584518110)
XLA Ops:
  0.6 117.9 %exchange.1 = (f32[2,256,3584]{2,1,0:T(8,128)S(1)}, bf16[32,16,3584]{2,1,0:T(8,128)(2,1)S(1)}, bf16[32,16,1024]{2,1,0:T(8,128)(2,1)S(1)}, f32[2,8]{1,0:T(2,128)S(1)}) custom-call(s32[2,8]{1,0:T(2,128)} %ids_hbm.1, f32[2,8]{1,0:T(2,128)} %weights_hbm.1, bf16[32,16,3584]{2,1,0:T(8,128)(2,1)} %fi_hbm.1, bf16[32,16,1024]{2,1,0:T(8,128)(2,1)} %fo_hbm.1, ...), custom_call_target="tpu_custom_call" | custom-call | tf_op jit(solution)/shard_map/exchange/pallas_call | solution.py:325
  118.5 4.5 %store.1 = (f32[2,256,3584]{2,1,0:T(8,128)}, bf16[32,16,3584]{2,1,0:T(8,128)(2,1)}, bf16[32,16,1024]{2,1,0:T(8,128)(2,1)}, f32[2,8]{1,0:T(2,128)}) custom-call(f32[2,256,3584]{2,1,0:T(8,128)S(1)} %get-tuple-element.12.refs_0_, bf16[32,16,3584]{2,1,0:T(8,128)(2,1)S(1)} %get-tuple-element.13.refs_1_, bf16[32,16,1024]{2,1,0:T(8,128)(2,1)S(1)} %get-tuple-element.14.refs_2_, ...), custom_call_target="tpu_custom_call" | custom-call | tf_op jit(solution)/shard_map/store/pallas_call | solution.py:378
